TPU v7x, 32 devices: a whole 2x2x4 slice. The times are simulated.
32 devices in a mesh: child: 4 (over y, x), shard: 8 (over z, core).
Axes of the slice: x: 2, y: 2, z: 4, core: 2. Of those that a mesh axis runs over, the one named last changes fastest.
Arguments:
- child_tensors: bfloat16 [4, 256, 256, 256], P('child', 'shard'), may hold values from -6 to 6
- leg_ops: bfloat16 [8, 256, 256], replicated, may hold values from -0.375 to 0.375
- term_ops: int32 [4, 4, 2], P('child'), may hold values from 0 to 7
- term_coef: float32 [4, 4], P('child'), may hold values from 0.5 to 1.5
- parent: bfloat16 [4, 256, 256], P('child', 'shard'), may hold values from -0.375 to 0.375
- top_env: float32 [256, 256], replicated, may hold values from -6 to 6
Outputs:
- applied: bfloat16 [4, 256, 256, 256], P('child', None, 'shard')
Inputs may be any that keep to these rules, and one draw needn't show every extreme that they name: `term_ops`: each entry names one of the 8 leg operators.
All inputs are finite; a program needn't handle non-finite values.
Results may differ from a plain program's by a relative error of at most 0.0091.
Values may be sent and summed in bfloat16 or wider, within the bound.
A program may use at most 128 MiB of HBM per device.

v0:
```python
import math
import jax
import jax.numpy as jnp
from jax import lax
from jax.sharding import PartitionSpec as P


def shards(child_tensors, leg_ops, term_ops, term_coef, parent, top_env):
    high = lax.Precision.HIGHEST
    tensor = child_tensors[0]
    bond = tensor.shape[1]
    picks = term_ops[0]
    weights = term_coef[0]
    number = weights.shape[0]
    onehot = (picks[:, :, None] == jnp.arange(leg_ops.shape[0])[None, None, :]).astype(jnp.bfloat16)
    chosen = jnp.einsum(
        "tjn,nab->tjab", onehot, leg_ops, preferred_element_type=jnp.float32
    ).astype(jnp.bfloat16)
    left_ops = chosen[:, 0]
    right_ops = chosen[:, 1]
    parent_block = parent[0]
    parent_full = lax.all_gather(parent_block, "shard", axis=0, tiled=True).astype(jnp.float32)
    regrouped = lax.all_to_all(tensor, "shard", split_axis=1, concat_axis=0, tiled=True)
    upward = lax.all_to_all(tensor, "shard", split_axis=2, concat_axis=0, tiled=True)
    summed = jnp.zeros((bond, bond, upward.shape[2]), jnp.float32)
    for term in range(number):
        image = jnp.einsum(
            "lru,rs->lsu", upward, right_ops[term], preferred_element_type=jnp.float32
        ).astype(jnp.bfloat16)
        summed = summed + weights[term] * jnp.einsum(
            "lk,lsu->ksu", left_ops[term], image, preferred_element_type=jnp.float32
        )
    local = lax.all_to_all(summed, "shard", split_axis=1, concat_axis=2, tiled=True)
    rounded = local.astype(jnp.bfloat16)
    env_part = (
        jnp.einsum("lsu,lsv->uv", regrouped, rounded, preferred_element_type=jnp.float32) / bond
    )
    block_rows = parent_block.astype(jnp.float32)
    env = lax.psum(env_part, "shard")
    lifted = jnp.dot(parent_full.T, jnp.dot(env, parent_full, precision=high), precision=high)
    total = lax.psum(lifted, "child")
    coupling = total - lifted + top_env
    factor = 1.0 / math.sqrt(bond * lax.axis_size("child"))
    partial_hole = (
        jnp.dot(jnp.dot(block_rows, coupling, precision=high), parent_full.T, precision=high)
        * factor
    )
    hole = lax.all_gather(partial_hole.astype(jnp.bfloat16), "shard", axis=0, tiled=True)
    result = local + jnp.einsum("lsu,uv->lsv", regrouped, hole, preferred_element_type=jnp.float32)
    return result.astype(jnp.bfloat16)[None]


def solution(mesh):
    in_specs = (
        P("child", "shard", None, None),
        P(),
        P("child", None, None),
        P("child", None),
        P("child", "shard", None),
        P(),
    )
    out_specs = P("child", None, "shard", None)
    return jax.shard_map(shards, mesh=mesh, in_specs=in_specs, out_specs=out_specs, check_vma=False)
```

profile of v0, /device:TPU:0, one launch (start us, length us, event | category | flops | bytes accessed | tf_op | source)
XLA Modules:
  0.0 548.4 jit_solution(6958713158814415964)
XLA Ops:
  6.5 8.0 %copy.56 = bf16[1,32,256,256]{2,1,3,0:T(8,128)(2,1)} copy(bf16[1,32,256,256]{3,2,1,0:T(8,128)(2,1)} %param.6) | data formatting | bytes 8388608 | tf_op args[0]
  14.5 6.4 %all-to-all-start = ((bf16[32,256,256]{1,0,2:T(8,128)(2,1)}), bf16[32,256,256]{1,0,2:T(8,128)(2,1)}, u32[]{:S(2)}, u32[]{:S(2)}) async-start(bf16[32,256,256]{1,0,2:T(8,128)(2,1)} %bitcast.131), calls=%async_computation | async-start | bytes 8388608 | tf_op jit(solution)/shard_map/all_to_all | solution.py:24
  20.9 6.6 %copy.78 = bf16[32,256,256]{2,0,1:T(8,128)(2,1)} copy(bf16[32,256,256]{2,1,0:T(8,128)(2,1)} %bitcast.130) | data formatting | bytes 8388608 | tf_op jit(solution)/shard_map/squeeze | solution.py:10
  27.4 87.5 %all-to-all-done = bf16[32,256,256]{1,0,2:T(8,128)(2,1)} async-done(((bf16[32,256,256]{1,0,2:T(8,128)(2,1)}), bf16[32,256,256]{1,0,2:T(8,128)(2,1)}, u32[]{:S(2)}, u32[]{:S(2)}) %all-to-all-start) | async-done | bytes 4194336 | tf_op jit(solution)/shard_map/all_to_all | solution.py:24
  114.9 4.6 all-to-all-start.2
  124.0 6.7 %copy.58 = bf16[8,32,256,32]{2,3,1,0:T(8,128)(2,1)} copy(bf16[8,32,256,32]{2,1,3,0:T(8,128)(2,1)} %bitcast.12) | data formatting | bytes 8388608 | tf_op jit(solution)/shard_map/all_to_all | solution.py:24
  130.7 9.6 %fusion.3 = f32[256,256,32]{1,0,2:T(8,128)} fusion(bf16[256,256,32]{1,2,0:T(8,128)(2,1)} %bitcast.126, bf16[1,1,256,256]{2,3,1,0:T(8,128)(2,1)S(1)} %copy.102, bf16[1,1,256,256]{2,3,1,0:T(8,128)(2,1)S(1)} %copy.101), kind=kOutput, calls=%fused_computation.5 | convolution fusion | flops 2149580800 | bytes 12845056 | tf_op jit(solution)/shard_map/lk,lsu->ksu/dot_general | solution.py:30
  140.3 9.6 %fusion.5 = f32[256,256,32]{1,0,2:T(8,128)} fusion(bf16[256,256,32]{1,2,0:T(8,128)(2,1)} %bitcast.127, bf16[1,1,256,256]{2,3,1,0:T(8,128)(2,1)S(1)} %copy.100, bf16[1,1,256,256]{2,3,1,0:T(8,128)(2,1)S(1)} %copy.99), kind=kOutput, calls=%fused_computation.7 | convolution fusion | flops 2149580800 | bytes 12845056 | tf_op jit(solution)/shard_map/lk,lsu->ksu/dot_general | solution.py:30
  149.9 9.9 %fusion.7 = f32[256,256,32]{1,0,2:T(8,128)} fusion(bf16[256,256,32]{1,2,0:T(8,128)(2,1)} %bitcast.128, bf16[1,1,256,256]{2,3,1,0:T(8,128)(2,1)S(1)} %copy.97, bf16[1,1,256,256]{2,3,1,0:T(8,128)(2,1)S(1)} %copy.96), kind=kOutput, calls=%fused_computation.9 | convolution fusion | flops 2149580800 | bytes 12845056 | tf_op jit(solution)/shard_map/lk,lsu->ksu/dot_general | solution.py:30
  159.8 19.6 %multiply_add_fusion = f32[256,256,32]{1,0,2:T(8,128)} fusion(f32[256,256,32]{1,0,2:T(8,128)} %fusion.3, f32[256,256,32]{1,0,2:T(8,128)} %fusion.5, f32[256,256,32]{1,0,2:T(8,128)} %fusion.7, f32[]{:T(128)} %bitcast.27, f32[]{:T(128)} %bitcast.21, f32[]{:T(128)} %bitcast.15, f32[]{:T(128)} %bitcast, bf16[256,256,32]{1,2,0:T(8,128)(2,1)} %bitcast.129, ...), kind=kOutput, calls=%fused_computation.2 | convolution fusion | flops 2164260864 | bytes 38010896 | tf_op jit(solution)/shard_map/lk,lsu->ksu/dot_general | solution.py:30
  179.4 10.3 %copy.75 = f32[256,256,32]{0,2,1:T(8,128)} copy(f32[256,256,32]{1,0,2:T(8,128)} %multiply_add_fusion) | data formatting | bytes 16777216 | tf_op jit(solution)/shard_map/add | solution.py:30
  189.7 23.8 %all-to-all-done.2 = bf16[32,256,256]{2,0,1:T(8,128)(2,1)} async-done(((bf16[32,256,256]{2,0,1:T(8,128)(2,1)}), bf16[32,256,256]{2,0,1:T(8,128)(2,1)}, u32[]{:S(2)}, u32[]{:S(2)}) %all-to-all-start.2) | async-done | bytes 4194336 | tf_op jit(solution)/shard_map/all_to_all | solution.py:23
  213.5 5.0 all-to-all-start.1
  218.5 4.8 copy.80
  223.4 179.0 %all-to-all-done.1 = f32[256,256,32]{0,2,1:T(8,128)} async-done(((f32[256,256,32]{0,2,1:T(8,128)}), f32[256,256,32]{0,2,1:T(8,128)}, u32[]{:S(2)}, u32[]{:S(2)}) %all-to-all-start.1) | async-done | bytes 8388640 | tf_op jit(solution)/shard_map/all_to_all | solution.py:33
  402.3 4.0 convert_element_type.51
  408.6 2.0 fusion.33
  410.6 14.4 %all-gather = bf16[1,256,256]{2,1,0:T(8,128)(2,1)S(1)} all-gather(bf16[1,32,256]{2,1,0:T(8,128)(2,1)S(1)} %copy-done.4), channel_id=2, replica_groups=mesh['child'=4,'shard'=8] {'shard'}, dimensions={1}, use_global_device_ids=true | all-gather | bytes 147456 | tf_op jit(solution)/shard_map/all_gather | solution.py:22
  425.0 40.1 %all-reduce.3.cloned.1.call-done = f32[256,256]{0,1:T(8,128)} async-done(((f32[256,256]{0,1:T(8,128)}), f32[256,256]{0,1:T(8,128)}) %all-reduce.3.cloned.1.call-update) | async-done | bytes 262160 | tf_op jit(solution)/shard_map/psum | solution.py:39
  467.7 8.3 %copy.76 = f32[256,32,8,32]{0,3,2,1:T(8,128)} copy(f32[256,32,8,32]{0,3,1,2:T(8,128)} %bitcast.34) | data formatting | bytes 16777216 | tf_op jit(solution)/shard_map/all_to_all | solution.py:33
  476.0 34.1 %all-reduce.5.cloned.1.call-done = f32[256,256]{0,1:T(8,128)} async-done(((f32[256,256]{0,1:T(8,128)}), f32[256,256]{0,1:T(8,128)}) %all-reduce.5.cloned.1.call-update) | async-done | bytes 262160 | tf_op jit(solution)/shard_map/psum | solution.py:41
  511.6 14.1 %all_gather.7 = bf16[256,256]{1,0:T(8,128)(2,1)S(1)} all-gather(bf16[32,256]{1,0:T(8,128)(2,1)S(1)} %fusion.34), channel_id=1, replica_groups=mesh['child'=4,'shard'=8] {'shard'}, dimensions={0}, use_global_device_ids=true | all-gather | bytes 147456 | tf_op jit(solution)/shard_map/all_gather | solution.py:48
  525.7 8.0 %fusion.31 = bf16[1,256,32,256]{1,3,2,0:T(8,128)(2,1)} fusion(bf16[256,32,256]{2,0,1:T(8,128)(2,1)} %bitcast.132, f32[256,32,8,32]{0,3,2,1:T(8,128)} %copy.76, bf16[256,256]{1,0:T(8,128)(2,1)S(1)} %all_gather.7), kind=kOutput, calls=%fused_computation.23 | convolution fusion | flops 1077936128 | bytes 16908288 | tf_op jit(solution)/shard_map/lsu,uv->lsv/dot_general | solution.py:49
  533.7 7.8 %copy.82 = bf16[1,256,32,256]{3,2,1,0:T(8,128)(2,1)} copy(bf16[1,256,32,256]{1,3,2,0:T(8,128)(2,1)} %fusion.31) | data formatting | bytes 8388608 | tf_op jit(solution)/shard_map/broadcast_in_dim | solution.py:50
  (35 shorter events, 10.8 us)
Async XLA Ops:
  14.5 100.4 %all-to-all-start = ((bf16[32,256,256]{1,0,2:T(8,128)(2,1)}), bf16[32,256,256]{1,0,2:T(8,128)(2,1)}, u32[]{:S(2)}, u32[]{:S(2)}) async-start(bf16[32,256,256]{1,0,2:T(8,128)(2,1)} %bitcast.131), calls=%async_computation | async-start | bytes 8388608 | tf_op jit(solution)/shard_map/all_to_all | solution.py:24
  27.4 92.1 %copy-start.2 = (bf16[8,256,256]{2,1,0:T(8,128)(2,1)S(1)}, bf16[8,256,256]{2,1,0:T(8,128)(2,1)}, u32[]{:S(2)}) copy-start(bf16[8,256,256]{2,1,0:T(8,128)(2,1)} %param.7) | copy-start | bytes 3145732
  27.4 92.1 %copy-start.6 = (s32[1,4,2]{1,2,0:T(2,128)S(1)}, s32[1,4,2]{1,2,0:T(2,128)}, u32[]{:S(2)}) copy-start(s32[1,4,2]{1,2,0:T(2,128)} %param.8) | copy-start | bytes 100
  114.9 98.6 %all-to-all-start.2 = ((bf16[32,256,256]{2,0,1:T(8,128)(2,1)}), bf16[32,256,256]{2,0,1:T(8,128)(2,1)}, u32[]{:S(2)}, u32[]{:S(2)}) async-start(bf16[32,256,256]{2,0,1:T(8,128)(2,1)} %copy.78), calls=%async_computation.2 | async-start | bytes 8388608 | tf_op jit(solution)/shard_map/all_to_all | solution.py:23
  120.4 2.9 copy-start.5
  213.5 188.8 %all-to-all-start.1 = ((f32[256,256,32]{0,2,1:T(8,128)}), f32[256,256,32]{0,2,1:T(8,128)}, u32[]{:S(2)}, u32[]{:S(2)}) async-start(f32[256,256,32]{0,2,1:T(8,128)} %copy.75), calls=%async_computation.1 | async-start | bytes 16777216 | tf_op jit(solution)/shard_map/all_to_all | solution.py:33
  218.5 246.6 %all-reduce.3.cloned.1.call-start = ((), (), s32[]{:S(2)}) async-start(), calls=%async_computation.3 | async-start | bytes 524288 | tf_op jit(solution)/shard_map/psum | solution.py:39
  406.4 2.2 copy-start
  408.6 2.1 copy-start.4
  408.6 59.0 %copy-start.3 = (f32[256,256]{1,0:T(8,128)S(1)}, f32[256,256]{1,0:T(8,128)}, u32[]{:S(2)}) copy-start(f32[256,256]{1,0:T(8,128)} %param.11) | copy-start | bytes 786436
  410.6 99.6 %all-reduce.5.cloned.1.call-start = ((), (), s32[]{:S(2)}) async-start(), calls=%async_computation.4 | async-start | bytes 524288 | tf_op jit(solution)/shard_map/psum | solution.py:41
  467.7 42.4 %copy-start.1 = (f32[256,256]{0,1:T(8,128)S(1)}, f32[256,256]{0,1:T(8,128)}, u32[]{:S(2)}) copy-start(f32[256,256]{0,1:T(8,128)} %convolution_bitcast_fusion) | copy-start | bytes 786436
Sparse Core Ops, SparseCore 0:
  410.7 54.3 all-reduce.2
  468.0 42.0 all-reduce.4
where the time goes:
time: 550 us; the launch traced here: 548 us
  waiting for transfers between devices  364 us (66%)
  matrix products  63.5 us (12%)
  local copies, waits for them, and re-layouts  58.4 us (11%)
  blocking collectives  28.4 us (5%)
  starting transfers between devices  16 us (3%)
  between operations  13.6 us (2%)
    all_to_all x1, waiting for transfers between devices, shards(): lax.all_to_all(summed, 'shard', split_axis=1, concat_axis=2, tiled=True)  179 us
    all_to_all x1, waiting for transfers between devices, shards(): lax.all_to_all(tensor, 'shard', split_axis=2, concat_axis=0, tiled=True)  87.5 us
    dot_general x4, matrix products, shards(): jnp.einsum('lk,lsu->ksu', left_ops[term], image, preferred_element_type=j...  48.7 us
    psum x1, waiting for transfers between devices, shards(): env = lax.psum(env_part, 'shard')  40.1 us
    psum x1, waiting for transfers between devices, shards(): total = lax.psum(lifted, 'child')  34.1 us
    all_to_all x1, waiting for transfers between devices, shards(): lax.all_to_all(tensor, 'shard', split_axis=1, concat_axis=0, tiled=True)  23.8 us
    all_gather x1, blocking collectives, shards(): lax.all_gather(parent_block, 'shard', axis=0, tiled=True)  14.4 us
    all_gather x1, blocking collectives, shards(): lax.all_gather(partial_hole.astype(jnp.bfloat16), 'shard', axis=0, tiled=...  14.1 us
  transfers between devices with their start and end apart: 5, of which 5 were waited for; matrix products, arithmetic and copies ran while one was open for 16% of the time, Pallas kernels for 0%

commit v1 on v0

--- a/solution.py
+++ b/solution.py
@@ -38,7 +38,8 @@
     block_rows = parent_block.astype(jnp.float32)
     env = lax.psum(env_part, "shard")
     lifted = jnp.dot(parent_full.T, jnp.dot(env, parent_full, precision=high), precision=high)
-    total = lax.psum(lifted, "child")
+    terms = lax.all_gather(lifted, "child")
+    total = jnp.sum(terms, axis=0)
     coupling = total - lifted + top_env
     factor = 1.0 / math.sqrt(bond * lax.axis_size("child"))
     partial_hole = (

time: 550 us -> 534 us (0.971)
  waiting for transfers between devices: 364 us -> 347 us
    psum x1 -> x0, waiting for transfers between devices: 34.1 us -> none  [shards(): total = lax.psum(lifted, 'child')]
    all_gather x0 -> x1, waiting for transfers between devices: none -> 17.1 us  [shards(): terms = lax.all_gather(lifted, 'child')]
  transfers between devices with their start and end apart: 5 -> 5, of which waited for: 5 -> 5; matrix products, arithmetic and copies ran while one was open for 16% -> 17% of each run, Pallas kernels for 0% -> 0%
where the time goes in v1:
time: 534 us; the launch traced here: 533 us
  waiting for transfers between devices  347 us (65%)
  matrix products  62.5 us (12%)
  local copies, waits for them, and re-layouts  60.1 us (11%)
  blocking collectives  28.4 us (5%)
  starting transfers between devices  16 us (3%)
  between operations  13.6 us (3%)
    all_to_all x1, waiting for transfers between devices, shards(): lax.all_to_all(summed, 'shard', split_axis=1, concat_axis=2, tiled=True)  179 us
    all_to_all x1, waiting for transfers between devices, shards(): lax.all_to_all(tensor, 'shard', split_axis=2, concat_axis=0, tiled=True)  87.5 us
    dot_general x4, matrix products, shards(): jnp.einsum('lk,lsu->ksu', left_ops[term], image, preferred_element_type=j...  48.7 us
    psum x1, waiting for transfers between devices, shards(): env = lax.psum(env_part, 'shard')  40.1 us
    all_to_all x1, waiting for transfers between devices, shards(): lax.all_to_all(tensor, 'shard', split_axis=1, concat_axis=0, tiled=True)  23.8 us
    all_gather x1, waiting for transfers between devices, shards(): terms = lax.all_gather(lifted, 'child')  17.1 us
    all_gather x1, blocking collectives, shards(): lax.all_gather(parent_block, 'shard', axis=0, tiled=True)  14.4 us
    all_gather x1, blocking collectives, shards(): lax.all_gather(partial_hole.astype(jnp.bfloat16), 'shard', axis=0, tiled=...  14.1 us
  transfers between devices with their start and end apart: 5, of which 5 were waited for; matrix products, arithmetic and copies ran while one was open for 17% of the time, Pallas kernels for 0%

profile of v1, /device:TPU:0, one launch (start us, length us, event | category | flops | bytes accessed | tf_op | source)
XLA Modules:
  0.0 532.8 jit_solution(16333844639123428774)
XLA Ops:
  6.5 8.0 %copy.56 = bf16[1,32,256,256]{2,1,3,0:T(8,128)(2,1)} copy(bf16[1,32,256,256]{3,2,1,0:T(8,128)(2,1)} %param.6) | data formatting | bytes 8388608 | tf_op args[0]
  14.5 6.4 %all-to-all-start = ((bf16[32,256,256]{1,0,2:T(8,128)(2,1)}), bf16[32,256,256]{1,0,2:T(8,128)(2,1)}, u32[]{:S(2)}, u32[]{:S(2)}) async-start(bf16[32,256,256]{1,0,2:T(8,128)(2,1)} %bitcast.133), calls=%async_computation | async-start | bytes 8388608 | tf_op jit(solution)/shard_map/all_to_all | solution.py:24
  20.9 6.6 %copy.78 = bf16[32,256,256]{2,0,1:T(8,128)(2,1)} copy(bf16[32,256,256]{2,1,0:T(8,128)(2,1)} %bitcast.132) | data formatting | bytes 8388608 | tf_op jit(solution)/shard_map/squeeze | solution.py:10
  27.4 87.5 %all-to-all-done = bf16[32,256,256]{1,0,2:T(8,128)(2,1)} async-done(((bf16[32,256,256]{1,0,2:T(8,128)(2,1)}), bf16[32,256,256]{1,0,2:T(8,128)(2,1)}, u32[]{:S(2)}, u32[]{:S(2)}) %all-to-all-start) | async-done | bytes 4194336 | tf_op jit(solution)/shard_map/all_to_all | solution.py:24
  114.9 4.6 all-to-all-start.2
  124.0 6.7 %copy.58 = bf16[8,32,256,32]{2,3,1,0:T(8,128)(2,1)} copy(bf16[8,32,256,32]{2,1,3,0:T(8,128)(2,1)} %bitcast.12) | data formatting | bytes 8388608 | tf_op jit(solution)/shard_map/all_to_all | solution.py:24
  130.7 9.6 %fusion.3 = f32[256,256,32]{1,0,2:T(8,128)} fusion(bf16[256,256,32]{1,2,0:T(8,128)(2,1)} %bitcast.128, bf16[1,1,256,256]{2,3,1,0:T(8,128)(2,1)S(1)} %copy.102, bf16[1,1,256,256]{2,3,1,0:T(8,128)(2,1)S(1)} %copy.101), kind=kOutput, calls=%fused_computation.5 | convolution fusion | flops 2149580800 | bytes 12845056 | tf_op jit(solution)/shard_map/lk,lsu->ksu/dot_general | solution.py:30
  140.3 9.6 %fusion.5 = f32[256,256,32]{1,0,2:T(8,128)} fusion(bf16[256,256,32]{1,2,0:T(8,128)(2,1)} %bitcast.129, bf16[1,1,256,256]{2,3,1,0:T(8,128)(2,1)S(1)} %copy.100, bf16[1,1,256,256]{2,3,1,0:T(8,128)(2,1)S(1)} %copy.99), kind=kOutput, calls=%fused_computation.7 | convolution fusion | flops 2149580800 | bytes 12845056 | tf_op jit(solution)/shard_map/lk,lsu->ksu/dot_general | solution.py:30
  149.9 9.9 %fusion.7 = f32[256,256,32]{1,0,2:T(8,128)} fusion(bf16[256,256,32]{1,2,0:T(8,128)(2,1)} %bitcast.130, bf16[1,1,256,256]{2,3,1,0:T(8,128)(2,1)S(1)} %copy.97, bf16[1,1,256,256]{2,3,1,0:T(8,128)(2,1)S(1)} %copy.96), kind=kOutput, calls=%fused_computation.9 | convolution fusion | flops 2149580800 | bytes 12845056 | tf_op jit(solution)/shard_map/lk,lsu->ksu/dot_general | solution.py:30
  159.8 19.6 %multiply_add_fusion = f32[256,256,32]{1,0,2:T(8,128)} fusion(f32[256,256,32]{1,0,2:T(8,128)} %fusion.3, f32[256,256,32]{1,0,2:T(8,128)} %fusion.5, f32[256,256,32]{1,0,2:T(8,128)} %fusion.7, f32[]{:T(128)} %bitcast.27, f32[]{:T(128)} %bitcast.21, f32[]{:T(128)} %bitcast.15, f32[]{:T(128)} %bitcast, bf16[256,256,32]{1,2,0:T(8,128)(2,1)} %bitcast.131, ...), kind=kOutput, calls=%fused_computation.2 | convolution fusion | flops 2164260864 | bytes 38010896 | tf_op jit(solution)/shard_map/lk,lsu->ksu/dot_general | solution.py:30
  179.4 10.3 %copy.75 = f32[256,256,32]{0,2,1:T(8,128)} copy(f32[256,256,32]{1,0,2:T(8,128)} %multiply_add_fusion) | data formatting | bytes 16777216 | tf_op jit(solution)/shard_map/add | solution.py:30
  189.7 23.8 %all-to-all-done.2 = bf16[32,256,256]{2,0,1:T(8,128)(2,1)} async-done(((bf16[32,256,256]{2,0,1:T(8,128)(2,1)}), bf16[32,256,256]{2,0,1:T(8,128)(2,1)}, u32[]{:S(2)}, u32[]{:S(2)}) %all-to-all-start.2) | async-done | bytes 4194336 | tf_op jit(solution)/shard_map/all_to_all | solution.py:23
  213.5 5.0 all-to-all-start.1
  218.5 4.8 copy.80
  223.4 179.0 %all-to-all-done.1 = f32[256,256,32]{0,2,1:T(8,128)} async-done(((f32[256,256,32]{0,2,1:T(8,128)}), f32[256,256,32]{0,2,1:T(8,128)}, u32[]{:S(2)}, u32[]{:S(2)}) %all-to-all-start.1) | async-done | bytes 8388640 | tf_op jit(solution)/shard_map/all_to_all | solution.py:33
  402.3 4.0 convert_element_type.51
  408.6 2.0 fusion.33
  410.6 14.4 %all-gather = bf16[1,256,256]{2,1,0:T(8,128)(2,1)S(1)} all-gather(bf16[1,32,256]{2,1,0:T(8,128)(2,1)S(1)} %copy-done.4), channel_id=2, replica_groups=mesh['child'=4,'shard'=8] {'shard'}, dimensions={1}, use_global_device_ids=true | all-gather | bytes 147456 | tf_op jit(solution)/shard_map/all_gather | solution.py:22
  425.0 40.1 %all-reduce.2.cloned.1.call-done = f32[256,256]{0,1:T(8,128)} async-done(((f32[256,256]{0,1:T(8,128)}), f32[256,256]{0,1:T(8,128)}) %all-reduce.2.cloned.1.call-update) | async-done | bytes 262160 | tf_op jit(solution)/shard_map/psum | solution.py:39
  467.7 8.3 %copy.76 = f32[256,32,8,32]{0,3,2,1:T(8,128)} copy(f32[256,32,8,32]{0,3,1,2:T(8,128)} %bitcast.34) | data formatting | bytes 16777216 | tf_op jit(solution)/shard_map/all_to_all | solution.py:33
  476.1 17.1 %all-gather.4.cloned.1.call-done = f32[1024,256]{0,1:T(8,128)} async-done(((f32[256,256]{0,1:T(8,128)}), f32[1024,256]{0,1:T(8,128)}) %all-gather.4.cloned.1.call-update) | async-done | bytes 1048592 | tf_op jit(solution)/shard_map/all_gather | solution.py:41
  496.0 14.1 %all_gather.15 = bf16[256,256]{1,0:T(8,128)(2,1)S(1)} all-gather(bf16[32,256]{1,0:T(8,128)(2,1)S(1)} %fusion.34), channel_id=1, replica_groups=mesh['child'=4,'shard'=8] {'shard'}, dimensions={0}, use_global_device_ids=true | all-gather | bytes 147456 | tf_op jit(solution)/shard_map/all_gather | solution.py:49
  510.1 8.0 %fusion.31 = bf16[1,256,32,256]{1,3,2,0:T(8,128)(2,1)} fusion(bf16[256,32,256]{2,0,1:T(8,128)(2,1)} %bitcast.134, f32[256,32,8,32]{0,3,2,1:T(8,128)} %copy.76, bf16[256,256]{1,0:T(8,128)(2,1)S(1)} %all_gather.15), kind=kOutput, calls=%fused_computation.23 | convolution fusion | flops 1077936128 | bytes 16908288 | tf_op jit(solution)/shard_map/lsu,uv->lsv/dot_general | solution.py:50
  518.1 7.8 %copy.82 = bf16[1,256,32,256]{3,2,1,0:T(8,128)(2,1)} copy(bf16[1,256,32,256]{1,3,2,0:T(8,128)(2,1)} %fusion.31) | data formatting | bytes 8388608 | tf_op jit(solution)/shard_map/broadcast_in_dim | solution.py:51
  (37 shorter events, 12.2 us)
Async XLA Ops:
  14.5 100.4 %all-to-all-start = ((bf16[32,256,256]{1,0,2:T(8,128)(2,1)}), bf16[32,256,256]{1,0,2:T(8,128)(2,1)}, u32[]{:S(2)}, u32[]{:S(2)}) async-start(bf16[32,256,256]{1,0,2:T(8,128)(2,1)} %bitcast.133), calls=%async_computation | async-start | bytes 8388608 | tf_op jit(solution)/shard_map/all_to_all | solution.py:24
  27.4 92.1 %copy-start.2 = (bf16[8,256,256]{2,1,0:T(8,128)(2,1)S(1)}, bf16[8,256,256]{2,1,0:T(8,128)(2,1)}, u32[]{:S(2)}) copy-start(bf16[8,256,256]{2,1,0:T(8,128)(2,1)} %param.7) | copy-start | bytes 3145732
  27.4 92.1 %copy-start.6 = (s32[1,4,2]{1,2,0:T(2,128)S(1)}, s32[1,4,2]{1,2,0:T(2,128)}, u32[]{:S(2)}) copy-start(s32[1,4,2]{1,2,0:T(2,128)} %param.8) | copy-start | bytes 100
  114.9 98.6 %all-to-all-start.2 = ((bf16[32,256,256]{2,0,1:T(8,128)(2,1)}), bf16[32,256,256]{2,0,1:T(8,128)(2,1)}, u32[]{:S(2)}, u32[]{:S(2)}) async-start(bf16[32,256,256]{2,0,1:T(8,128)(2,1)} %copy.78), calls=%async_computation.2 | async-start | bytes 8388608 | tf_op jit(solution)/shard_map/all_to_all | solution.py:23
  120.4 2.9 copy-start.5
  213.5 188.8 %all-to-all-start.1 = ((f32[256,256,32]{0,2,1:T(8,128)}), f32[256,256,32]{0,2,1:T(8,128)}, u32[]{:S(2)}, u32[]{:S(2)}) async-start(f32[256,256,32]{0,2,1:T(8,128)} %copy.75), calls=%async_computation.1 | async-start | bytes 16777216 | tf_op jit(solution)/shard_map/all_to_all | solution.py:33
  218.5 246.6 %all-reduce.2.cloned.1.call-start = ((), (), s32[]{:S(2)}) async-start(), calls=%async_computation.3 | async-start | bytes 524288 | tf_op jit(solution)/shard_map/psum | solution.py:39
  406.4 2.2 copy-start
  408.6 2.1 copy-start.4
  408.6 59.0 %copy-start.3 = (f32[256,256]{1,0:T(8,128)S(1)}, f32[256,256]{1,0:T(8,128)}, u32[]{:S(2)}) copy-start(f32[256,256]{1,0:T(8,128)} %param.11) | copy-start | bytes 786436
  410.6 82.6 %all-gather.4.cloned.1.call-start = ((), (), s32[]{:S(2)}) async-start(), calls=%async_computation.4 | async-start | bytes 1310720 | tf_op jit(solution)/shard_map/all_gather | solution.py:41
  467.7 27.7 %copy-start.1 = (f32[256,256]{0,1:T(8,128)S(1)}, f32[256,256]{0,1:T(8,128)}, u32[]{:S(2)}) copy-start(f32[256,256]{0,1:T(8,128)} %convolution_bitcast_fusion) | copy-start | bytes 786436
Sparse Core Ops, SparseCore 0:
  410.7 54.3 all-reduce.1
  467.7 25.4 all-gather.3
